TPU v7x, 512 devices: a whole 4x8x8 slice. The times are simulated.
512 devices in a mesh: row: 64 (over z, y), bundle: 8 (over x, core).
Axes of the slice: x: 4, y: 8, z: 8, core: 2. Of those that a mesh axis runs over, the one named last changes fastest.
Arguments:
- vectors: float32 [256, 131072], P('bundle', 'row'), may hold values from -6 to 6
- blocks: float32 [2048, 64, 384], P('row'), may hold values from -0.30618622 to 0.30618622, as said below
- columns: int32 [2048, 6], P('row'), may hold values from 0 to 2047, as said below
- bounds: float32 [2], replicated, may hold values from -0.9 to 0.5, as said below
Outputs:
- basis: float32 [256, 131072], P(None, ('row', 'bundle'))
- factor: float32 [256, 256], replicated
Inputs may be any that keep to these rules, and one draw needn't show every extreme that they name: Slot 0 of block row i is i itself; every block column of block row i lies within 32 block rows of i, counted cyclically over the 2048 block rows, and a distance of exactly 32 occurs; columns of one block row may repeat. `blocks`: together with columns they make H symmetric. bounds[0] < 0 < bounds[1].
All inputs are finite; a program needn't handle non-finite values.
Results may differ from a plain program's by a relative error of at most 0.00011.
Values sent between devices are 32-bit elements; how exact they have to be, the bound alone decides.
No kernel may reach another device: no remote copies, remote signals or barrier semaphores. Data moves between devices by JAX's collectives and lax.ppermute only.
A program may use at most 64 MiB of HBM per device.

v0:
```python
import jax
import jax.numpy as jnp
from jax import lax
from jax.sharding import PartitionSpec as P


def extended_2(block, sides, width):
    for axis, dim in sides:
        count = lax.axis_size(axis)
        forward = [(i, i + 1) for i in range(count - 1)]
        forward.append((count - 1, 0))
        backward = [(target, source) for source, target in forward]
        low = lax.ppermute(
            lax.slice_in_dim(block, block.shape[dim] - width, None, axis=dim), axis, forward
        )
        high = lax.ppermute(lax.slice_in_dim(block, 0, width, axis=dim), axis, backward)
        block = jnp.concatenate([low, block, high], axis=dim)
    return block


def local(vectors, blocks, columns, bounds):
    block_rows = blocks.shape[0]
    block_size = blocks.shape[1]
    slot_count = columns.shape[1]
    row_count = lax.axis_size("row")
    total_rows = block_rows * row_count
    first_row = lax.axis_index("row") * block_rows
    center = (bounds[0] + bounds[1]) * 0.5
    half = (bounds[1] - bounds[0]) * 0.5
    local_cols = jnp.mod(columns - first_row + block_rows, total_rows).reshape(-1)

    def apply_operator(field):
        extended = extended_2(field, (("row", 1),), block_rows * block_size)
        width = field.shape[0]
        extended3 = extended.reshape(width, 3 * block_rows, block_size)
        picked = jnp.take(extended3, local_cols, axis=1).reshape(
            width, block_rows, slot_count * block_size
        )
        result = jnp.einsum("iam,cim->cia", blocks, picked, precision=lax.Precision.HIGHEST)
        return result.reshape(width, block_rows * block_size)

    first = (apply_operator(vectors) - center * vectors) / half
    second = 2.0 * (apply_operator(first) - center * first) / half - vectors
    filtered = 2.0 * (apply_operator(second) - center * second) / half - first
    stacked = lax.all_to_all(filtered, "bundle", split_axis=1, concat_axis=0, tiled=True)
    gram = jnp.dot(
        stacked, stacked.T, precision=lax.Precision.HIGHEST, preferred_element_type=jnp.float32
    )
    gram = lax.psum(gram, ("row", "bundle"))
    lower = jnp.linalg.cholesky(gram)
    basis = jax.scipy.linalg.solve_triangular(lower, stacked, lower=True)
    return (basis, lower.T)


def solution(mesh):
    placed = (P("bundle", "row"), P("row", None, None), P("row", None), P())
    return jax.shard_map(
        local,
        mesh=mesh,
        in_specs=placed,
        out_specs=(P(None, ("row", "bundle")), P()),
        check_vma=False,
    )
```

profile of v0, /device:TPU:23, one launch (start us, length us, event | category | flops | bytes accessed | tf_op | source)
XLA Modules:
  0.0 516.4 jit_solution(1491135728791172816)
XLA Ops:
  17.6 3.5 collective-permute-done.1
  26.0 3.5 copy.10
  29.5 3.8 gather_fusion
  38.9 3.8 reshape.71
  42.7 5.6 %fusion.6 = f32[32,32,64]{2,0,1:T(8,128)S(1)} fusion(f32[32,64,384]{2,1,0:T(8,128)S(1)} %copy-done, f32[32,32,384]{2,1,0:T(8,128)} %reshape.71), kind=kOutput, calls=%fused_computation.14 | convolution fusion | flops 301989888 | bytes 4980736 | tf_op jit(solution)/shard_map/iam,cim->cia/dot_general | solution.py:39
  52.4 4.3 collective-permute-start.2
  60.6 3.7 collective-permute-done.3
  68.2 3.5 copy.14
  71.7 3.8 gather_fusion.1
  81.1 3.8 reshape.74
  84.9 5.6 %fusion.9 = f32[32,32,64]{2,0,1:T(8,128)S(1)} fusion(f32[32,64,384]{2,1,0:T(8,128)S(1)} %copy-done, f32[32,32,384]{2,1,0:T(8,128)} %reshape.74), kind=kOutput, calls=%fused_computation.15 | convolution fusion | flops 301989888 | bytes 4980736 | tf_op jit(solution)/shard_map/iam,cim->cia/dot_general | solution.py:39
  98.1 4.0 collective-permute-start.5
  109.3 3.5 copy.18
  112.8 3.8 gather_fusion.2
  122.2 3.8 reshape.77
  126.0 5.6 %fusion.12 = f32[32,32,64]{2,0,1:T(8,128)S(1)} fusion(f32[32,64,384]{2,1,0:T(8,128)S(1)} %copy-done, f32[32,32,384]{2,1,0:T(8,128)} %reshape.77), kind=kOutput, calls=%fused_computation.16 | convolution fusion | flops 301989888 | bytes 4980736 | tf_op jit(solution)/shard_map/iam,cim->cia/dot_general | solution.py:39
  136.5 8.2 %all-to-all-start = ((f32[32,8,256]{2,0,1:T(8,128)}), f32[32,8,256]{2,0,1:T(8,128)S(1)}, u32[]{:S(2)}, u32[]{:S(2)}) async-start(f32[32,8,256]{2,0,1:T(8,128)} %bitcast.65), calls=%async_computation | async-start | bytes 524288 | tf_op jit(solution)/shard_map/all_to_all | solution.py:45
  144.9 4.6 all-to-all-done
  151.3 277.9 %all-reduce.3.cloned.1.call-done = f32[256,256]{0,1:T(8,128)} async-done(((f32[256,256]{0,1:T(8,128)}), f32[256,256]{0,1:T(8,128)}) %all-reduce.3.cloned.1.call-update) | async-done | bytes 262160 | tf_op jit(solution)/shard_map/psum | solution.py:49
  431.9 11.7 %cholesky.50 = f32[128,128]{1,0:T(8,128)S(1)} custom-call(f32[128,128]{1,0:T(8,128)S(1)} %cholesky.118), custom_call_target="Cholesky" | custom-call | tf_op jit(solution)/shard_map/jit(cholesky)/cholesky | solution.py:50
  445.8 11.3 %custom-call.15 = f32[1,128,128]{1,2,0:T(8,128)} custom-call(f32[1,128,128]{2,1,0:T(8,128)} %get-tuple-element.32), custom_call_target="InvertDiagBlocksLowerTriangular" | custom-call | tf_op jit(solution)/shard_map/jit(cholesky)/cholesky | solution.py:50
  459.8 13.2 %cholesky.105 = f32[128,128]{1,0:T(8,128)} custom-call(f32[128,128]{1,0:T(8,128)} %convolution_subtract_fusion.1), custom_call_target="Cholesky" | custom-call | tf_op jit(solution)/shard_map/jit(cholesky)/cholesky | solution.py:50
  477.7 5.3 %while.1 = (s32[]{:T(128)}, f32[256,256]{1,0:T(8,128)S(1)}, s32[2,2]{1,0:T(2,128)S(1)}, f32[2,128,128]{2,1,0:T(8,128)}, s32[]{:T(128)}) while((s32[]{:T(128)}, f32[256,256]{1,0:T(8,128)S(1)}, s32[2,2]{1,0:T(2,128)S(1)}, f32[2,128,128]{2,1,0:T(8,128)}, s32[]{:T(128)}) %tuple.33), condition=%wide.while_cond, body=%wide.while_body.sunk | while | flops 2 | bytes 132705 | solution.py:51
  482.9 21.1 %custom-call.16 = f32[2,128,128]{1,2,0:T(8,128)} custom-call(f32[2,128,128]{2,1,0:T(8,128)} %get-tuple-element.10), custom_call_target="InvertDiagBlocksLowerTriangular" | custom-call | tf_op jit(solution)/shard_map/jit(_solve_triangular)/triangular_solve | solution.py:51
  (75 shorter events, 84.3 us)
Async XLA Ops:
  7.2 35.5 %copy-start = (f32[32,64,384]{2,1,0:T(8,128)S(1)}, f32[32,64,384]{2,1,0:T(8,128)}, u32[]{:S(2)}) copy-start(f32[32,64,384]{2,1,0:T(8,128)} %param.7) | copy-start | bytes 9437188
  7.2 10.4 %collective-permute-start = (f32[32,2048]{1,0:T(8,128)}, f32[32,2048]{1,0:T(8,128)S(1)}, u32[]{:S(2)}, u32[]{:S(2)}) collective-permute-start(f32[32,2048]{1,0:T(8,128)} %param.6), channel_id=1, source_target_pairs={{0,8},{8,16},{16,24},{24,32},{32,40},{40,48},{48,56},{56,64},{64,7... | collective-permute-start | bytes 786440 | tf_op jit(solution)/shard_map/ppermute | solution.py:13
  10.7 10.5 %collective-permute-start.1 = (f32[32,2048]{1,0:T(8,128)}, f32[32,2048]{1,0:T(8,128)}, u32[]{:S(2)}, u32[]{:S(2)}) collective-permute-start(f32[32,2048]{1,0:T(8,128)} %param.6), channel_id=1, source_target_pairs={{8,0},{16,8},{24,16},{32,24},{40,32},{48,40},{56,48},{64,56},{72,6... | collective-permute-start | bytes 786440 | tf_op jit(solution)/shard_map/ppermute | solution.py:16
  52.4 8.2 %collective-permute-start.2 = (f32[32,2048]{1,0:T(8,128)S(1)}, f32[32,2048]{1,0:T(8,128)S(1)}, u32[]{:S(2)}, u32[]{:S(2)}) collective-permute-start(f32[32,2048]{1,0:T(8,128)S(1)} %subtract_divide_fusion), channel_id=1, source_target_pairs={{0,8},{8,16},{16,24},{24,32},{32,40},{40,48},{48,56},{56,64},{64,7... | collective-permute-start | bytes 786440 | tf_op jit(solution)/shard_map/ppermute | solution.py:13
  56.7 7.7 %collective-permute-start.3 = (f32[32,2048]{1,0:T(8,128)S(1)}, f32[32,2048]{1,0:T(8,128)S(1)}, u32[]{:S(2)}, u32[]{:S(2)}) collective-permute-start(f32[32,2048]{1,0:T(8,128)S(1)} %subtract_divide_fusion), channel_id=1, source_target_pairs={{8,0},{16,8},{24,16},{32,24},{40,32},{48,40},{56,48},{64,56},{72,6... | collective-permute-start | bytes 786440 | tf_op jit(solution)/shard_map/ppermute | solution.py:16
  94.6 10.8 %copy-start.1 = (f32[32,2048]{1,0:T(8,128)}, f32[32,2048]{1,0:T(8,128)S(1)}, u32[]{:S(2)}) copy-start(f32[32,2048]{1,0:T(8,128)S(1)} %divide_subtract_fusion.1) | copy-start | bytes 786436
  94.6 9.7 %collective-permute-start.4 = (f32[32,2048]{1,0:T(8,128)S(1)}, f32[32,2048]{1,0:T(8,128)S(1)}, u32[]{:S(2)}, u32[]{:S(2)}) collective-permute-start(f32[32,2048]{1,0:T(8,128)S(1)} %divide_subtract_fusion.1), channel_id=1, source_target_pairs={{0,8},{8,16},{16,24},{24,32},{32,40},{40,48},{48,56},{56,64},{64,7... | collective-permute-start | bytes 786440 | tf_op jit(solution)/shard_map/ppermute | solution.py:13
  98.1 7.4 %collective-permute-start.5 = (f32[32,2048]{1,0:T(8,128)S(1)}, f32[32,2048]{1,0:T(8,128)S(1)}, u32[]{:S(2)}, u32[]{:S(2)}) collective-permute-start(f32[32,2048]{1,0:T(8,128)S(1)} %divide_subtract_fusion.1), channel_id=1, source_target_pairs={{8,0},{16,8},{24,16},{32,24},{40,32},{48,40},{56,48},{64,56},{72,6... | collective-permute-start | bytes 786440 | tf_op jit(solution)/shard_map/ppermute | solution.py:16
  136.5 13.0 %all-to-all-start = ((f32[32,8,256]{2,0,1:T(8,128)}), f32[32,8,256]{2,0,1:T(8,128)S(1)}, u32[]{:S(2)}, u32[]{:S(2)}) async-start(f32[32,8,256]{2,0,1:T(8,128)} %bitcast.65), calls=%async_computation | async-start | bytes 524288 | tf_op jit(solution)/shard_map/all_to_all | solution.py:45
  144.7 284.5 %all-reduce.3.cloned.1.call-start = ((), (), s32[]{:S(2)}) async-start(), calls=%async_computation.1 | async-start | bytes 524288 | tf_op jit(solution)/shard_map/psum | solution.py:49
  431.2 0.7 copy-start.3
  443.6 0.6 copy-start.4
  473.9 2.0 copy-start.2
Sparse Core Ops, SparseCore 0:
  151.0 278.0 all-reduce.2
where the time goes:
time: 525 us; the launch traced here: 516 us
  waiting for transfers between devices  295 us (56%)
  other arithmetic  77.2 us (15%)
  local copies, waits for them, and re-layouts  74.4 us (14%)
  starting transfers between devices  28.1 us (5%)
  matrix products  23.4 us (4%)
  between operations  18.4 us (4%)
    psum x1, waiting for transfers between devices, local(): gram = lax.psum(gram, ('row', 'bundle'))  278 us
    another operation x6, other arithmetic, local(): lower = jnp.linalg.cholesky(gram)  38.4 us
    another operation x3, other arithmetic, local(): basis = jax.scipy.linalg.solve_triangular(lower, stacked, lower=True)  21.8 us
    reshape x6, local copies, waits for them, and re-layouts, apply_operator(): extended3 = extended.reshape(width, 3 * block_rows, block_size)  19.2 us
    dot_general x3, matrix products, apply_operator(): jnp.einsum('iam,cim->cia', blocks, picked, precision=lax.Precision.HIGHEST)  16.8 us
    gather x3, local copies, waits for them, and re-layouts, apply_operator(): jnp.take(extended3, local_cols, axis=1)  11.4 us
    reshape x3, local copies, waits for them, and re-layouts, apply_operator(): jnp.take(extended3, local_cols, axis=1)  11.3 us
    ppermute x3, starting transfers between devices, extended_2(): lax.ppermute(lax.slice_in_dim(block, block.shape[dim] - width, None, axis...  11.2 us
  transfers between devices with their start and end apart: 8, of which 7 were waited for; matrix products, arithmetic and copies ran while one was open for 1% of the time, Pallas kernels for 0%

commit v1 on v0

--- a/solution.py
+++ b/solution.py
@@ -1,7 +1,15 @@
+import functools
 import jax
 import jax.numpy as jnp
 from jax import lax
 from jax.sharding import PartitionSpec as P
+
+
+def number_the_squares(local_x, mesh_dim, named_axis):
+    return jax.lax.psum(jax.lax.psum(local_x, axis_name=mesh_dim), axis_name=named_axis)
+
+
+pairs_all_replace = functools.partial(number_the_squares, mesh_dim="row", named_axis="bundle")
 
 
 def extended_2(block, sides, width):
@@ -46,7 +54,7 @@
     gram = jnp.dot(
         stacked, stacked.T, precision=lax.Precision.HIGHEST, preferred_element_type=jnp.float32
     )
-    gram = lax.psum(gram, ("row", "bundle"))
+    gram = pairs_all_replace(gram)
     lower = jnp.linalg.cholesky(gram)
     basis = jax.scipy.linalg.solve_triangular(lower, stacked, lower=True)
     return (basis, lower.T)

time: 525 us -> 476 us (0.907)
  the two profiles are of different devices: /device:TPU:23 before, /device:TPU:8 now
where the time goes in v1:
time: 476 us; the launch traced here: 467 us
  waiting for transfers between devices  230 us (48%)
  other arithmetic  77.2 us (16%)
  local copies, waits for them, and re-layouts  74 us (16%)
  starting transfers between devices  31.9 us (7%)
  matrix products  23.4 us (5%)
  between operations  18.5 us (4%)
  blocking collectives  11.6 us (2%)
    psum x1, waiting for transfers between devices, number_the_squares(): jax.lax.psum(local_x, axis_name=mesh_dim)  153 us
    psum x1, waiting for transfers between devices, number_the_squares(): jax.lax.psum(jax.lax.psum(local_x, axis_name=mesh_dim), axis_name=named_a...  69.5 us
    another operation x6, other arithmetic, local(): lower = jnp.linalg.cholesky(gram)  38.4 us
    ppermute x3, starting transfers between devices, extended_2(): lax.ppermute(lax.slice_in_dim(block, 0, width, axis=dim), axis, backward)  22.5 us
    another operation x3, other arithmetic, local(): basis = jax.scipy.linalg.solve_triangular(lower, stacked, lower=True)  21.8 us
    reshape x6, local copies, waits for them, and re-layouts, apply_operator(): extended3 = extended.reshape(width, 3 * block_rows, block_size)  19.2 us
    dot_general x3, matrix products, apply_operator(): jnp.einsum('iam,cim->cia', blocks, picked, precision=lax.Precision.HIGHEST)  16.8 us
    all_to_all x1, blocking collectives, local(): lax.all_to_all(filtered, 'bundle', split_axis=1, concat_axis=0, tiled=True)  11.6 us
  transfers between devices with their start and end apart: 8, of which 6 were waited for; matrix products, arithmetic and copies ran while one was open for 1% of the time, Pallas kernels for 0%

profile of v1, /device:TPU:8, one launch (start us, length us, event | category | flops | bytes accessed | tf_op | source)
XLA Modules:
  0.0 467.1 jit_solution(12348188963206577727)
XLA Ops:
  7.2 3.8 collective-permute-start
  11.0 6.1 %collective-permute-start.1 = (f32[32,2048]{1,0:T(8,128)}, f32[32,2048]{1,0:T(8,128)}, u32[]{:S(2)}, u32[]{:S(2)}) collective-permute-start(f32[32,2048]{1,0:T(8,128)} %param.6), channel_id=1, source_target_pairs={{8,0},{16,8},{24,16},{32,24},{40,32},{48,40},{56,48},{64,56},{72,6... | collective-permute-start | bytes 786440 | tf_op jit(solution)/shard_map/ppermute | solution.py:24
  30.4 3.8 gather_fusion
  39.8 3.8 reshape.71
  43.6 5.6 %fusion.6 = f32[32,32,64]{2,0,1:T(8,128)S(1)} fusion(f32[32,64,384]{2,1,0:T(8,128)S(1)} %copy-done, f32[32,32,384]{2,1,0:T(8,128)} %reshape.71), kind=kOutput, calls=%fused_computation.14 | convolution fusion | flops 301989888 | bytes 4980736 | tf_op jit(solution)/shard_map/iam,cim->cia/dot_general | solution.py:47
  53.3 3.5 collective-permute-start.2
  56.8 8.4 %collective-permute-start.3 = (f32[32,2048]{1,0:T(8,128)S(1)}, f32[32,2048]{1,0:T(8,128)S(1)}, u32[]{:S(2)}, u32[]{:S(2)}) collective-permute-start(f32[32,2048]{1,0:T(8,128)S(1)} %subtract_divide_fusion), channel_id=1, source_target_pairs={{8,0},{16,8},{24,16},{32,24},{40,32},{48,40},{56,48},{64,56},{72,6... | collective-permute-start | bytes 786440 | tf_op jit(solution)/shard_map/ppermute | solution.py:24
  73.3 3.5 copy.14
  76.8 3.8 gather_fusion.1
  86.3 3.8 reshape.74
  90.0 5.6 %fusion.9 = f32[32,32,64]{2,0,1:T(8,128)S(1)} fusion(f32[32,64,384]{2,1,0:T(8,128)S(1)} %copy-done, f32[32,32,384]{2,1,0:T(8,128)} %reshape.74), kind=kOutput, calls=%fused_computation.15 | convolution fusion | flops 301989888 | bytes 4980736 | tf_op jit(solution)/shard_map/iam,cim->cia/dot_general | solution.py:47
  101.7 7.9 %collective-permute-start.5 = (f32[32,2048]{1,0:T(8,128)S(1)}, f32[32,2048]{1,0:T(8,128)S(1)}, u32[]{:S(2)}, u32[]{:S(2)}) collective-permute-start(f32[32,2048]{1,0:T(8,128)S(1)} %divide_subtract_fusion.1), channel_id=1, source_target_pairs={{8,0},{16,8},{24,16},{32,24},{40,32},{48,40},{56,48},{64,56},{72,6... | collective-permute-start | bytes 786440 | tf_op jit(solution)/shard_map/ppermute | solution.py:24
  117.2 3.5 copy.18
  120.6 3.8 gather_fusion.2
  130.1 3.8 reshape.77
  133.9 5.6 %fusion.12 = f32[32,32,64]{2,0,1:T(8,128)S(1)} fusion(f32[32,64,384]{2,1,0:T(8,128)S(1)} %copy-done, f32[32,32,384]{2,1,0:T(8,128)} %reshape.77), kind=kOutput, calls=%fused_computation.16 | convolution fusion | flops 301989888 | bytes 4980736 | tf_op jit(solution)/shard_map/iam,cim->cia/dot_general | solution.py:47
  143.7 11.6 %all_to_all.19 = f32[32,8,256]{2,0,1:T(8,128)S(1)} all-to-all(f32[32,8,256]{2,0,1:T(8,128)S(1)} %bitcast.65), channel_id=1, replica_groups=mesh['row'=64,'bundle'=8] {'bundle'}, dimensions={1} | all-to-all | bytes 524288 | tf_op jit(solution)/shard_map/all_to_all | solution.py:53
  156.7 152.8 %all-reduce.4.cloned.1.call-done = f32[256,256]{0,1:T(8,128)} async-done(((f32[256,256]{0,1:T(8,128)}), f32[256,256]{0,1:T(8,128)}) %all-reduce.4.cloned.1.call-update) | async-done | bytes 262160 | tf_op jit(solution)/shard_map/psum | solution.py:9
  310.2 69.5 %all-reduce.6.cloned.1.call-done = f32[256,256]{0,1:T(8,128)} async-done(((f32[256,256]{0,1:T(8,128)}), f32[256,256]{0,1:T(8,128)}) %all-reduce.6.cloned.1.call-update) | async-done | bytes 262160 | tf_op jit(solution)/shard_map/psum | solution.py:9
  382.5 11.7 %cholesky.50 = f32[128,128]{1,0:T(8,128)S(1)} custom-call(f32[128,128]{1,0:T(8,128)S(1)} %cholesky.118), custom_call_target="Cholesky" | custom-call | tf_op jit(solution)/shard_map/jit(cholesky)/cholesky | solution.py:58
  396.3 11.3 %custom-call.15 = f32[1,128,128]{1,2,0:T(8,128)} custom-call(f32[1,128,128]{2,1,0:T(8,128)} %get-tuple-element.32), custom_call_target="InvertDiagBlocksLowerTriangular" | custom-call | tf_op jit(solution)/shard_map/jit(cholesky)/cholesky | solution.py:58
  410.4 13.2 %cholesky.105 = f32[128,128]{1,0:T(8,128)} custom-call(f32[128,128]{1,0:T(8,128)} %convolution_subtract_fusion.1), custom_call_target="Cholesky" | custom-call | tf_op jit(solution)/shard_map/jit(cholesky)/cholesky | solution.py:58
  428.3 5.4 %while.1 = (s32[]{:T(128)}, f32[256,256]{1,0:T(8,128)S(1)}, s32[2,2]{1,0:T(2,128)S(1)}, f32[2,128,128]{2,1,0:T(8,128)}, s32[]{:T(128)}) while((s32[]{:T(128)}, f32[256,256]{1,0:T(8,128)S(1)}, s32[2,2]{1,0:T(2,128)S(1)}, f32[2,128,128]{2,1,0:T(8,128)}, s32[]{:T(128)}) %tuple.33), condition=%wide.while_cond, body=%wide.while_body.sunk | while | flops 2 | bytes 132705 | solution.py:59
  433.7 21.1 %custom-call.16 = f32[2,128,128]{1,2,0:T(8,128)} custom-call(f32[2,128,128]{2,1,0:T(8,128)} %get-tuple-element.10), custom_call_target="InvertDiagBlocksLowerTriangular" | custom-call | tf_op jit(solution)/shard_map/jit(_solve_triangular)/triangular_solve | solution.py:59
  (77 shorter events, 80.9 us)
Async XLA Ops:
  7.2 36.4 %copy-start = (f32[32,64,384]{2,1,0:T(8,128)S(1)}, f32[32,64,384]{2,1,0:T(8,128)}, u32[]{:S(2)}) copy-start(f32[32,64,384]{2,1,0:T(8,128)} %param.7) | copy-start | bytes 9437188
  7.2 302.3 %all-reduce.4.cloned.1.call-start = ((), (), s32[]{:S(2)}) async-start(), calls=%async_computation.1 | async-start | bytes 524288 | tf_op jit(solution)/shard_map/psum | solution.py:9
  7.2 14.7 %collective-permute-start = (f32[32,2048]{1,0:T(8,128)}, f32[32,2048]{1,0:T(8,128)S(1)}, u32[]{:S(2)}, u32[]{:S(2)}) collective-permute-start(f32[32,2048]{1,0:T(8,128)} %param.6), channel_id=1, source_target_pairs={{0,8},{8,16},{16,24},{24,32},{32,40},{40,48},{48,56},{56,64},{64,7... | collective-permute-start | bytes 786440 | tf_op jit(solution)/shard_map/ppermute | solution.py:21
  11.0 11.0 %collective-permute-start.1 = (f32[32,2048]{1,0:T(8,128)}, f32[32,2048]{1,0:T(8,128)}, u32[]{:S(2)}, u32[]{:S(2)}) collective-permute-start(f32[32,2048]{1,0:T(8,128)} %param.6), channel_id=1, source_target_pairs={{8,0},{16,8},{24,16},{32,24},{40,32},{48,40},{56,48},{64,56},{72,6... | collective-permute-start | bytes 786440 | tf_op jit(solution)/shard_map/ppermute | solution.py:24
  53.3 14.9 %collective-permute-start.2 = (f32[32,2048]{1,0:T(8,128)S(1)}, f32[32,2048]{1,0:T(8,128)S(1)}, u32[]{:S(2)}, u32[]{:S(2)}) collective-permute-start(f32[32,2048]{1,0:T(8,128)S(1)} %subtract_divide_fusion), channel_id=1, source_target_pairs={{0,8},{8,16},{16,24},{24,32},{32,40},{40,48},{48,56},{56,64},{64,7... | collective-permute-start | bytes 786440 | tf_op jit(solution)/shard_map/ppermute | solution.py:21
  56.8 12.6 %collective-permute-start.3 = (f32[32,2048]{1,0:T(8,128)S(1)}, f32[32,2048]{1,0:T(8,128)S(1)}, u32[]{:S(2)}, u32[]{:S(2)}) collective-permute-start(f32[32,2048]{1,0:T(8,128)S(1)} %subtract_divide_fusion), channel_id=1, source_target_pairs={{8,0},{16,8},{24,16},{32,24},{40,32},{48,40},{56,48},{64,56},{72,6... | collective-permute-start | bytes 786440 | tf_op jit(solution)/shard_map/ppermute | solution.py:24
  99.8 13.5 %copy-start.1 = (f32[32,2048]{1,0:T(8,128)}, f32[32,2048]{1,0:T(8,128)S(1)}, u32[]{:S(2)}) copy-start(f32[32,2048]{1,0:T(8,128)S(1)} %divide_subtract_fusion.1) | copy-start | bytes 786436
  99.8 12.3 %collective-permute-start.4 = (f32[32,2048]{1,0:T(8,128)S(1)}, f32[32,2048]{1,0:T(8,128)S(1)}, u32[]{:S(2)}, u32[]{:S(2)}) collective-permute-start(f32[32,2048]{1,0:T(8,128)S(1)} %divide_subtract_fusion.1), channel_id=1, source_target_pairs={{0,8},{8,16},{16,24},{24,32},{32,40},{40,48},{48,56},{56,64},{64,7... | collective-permute-start | bytes 786440 | tf_op jit(solution)/shard_map/ppermute | solution.py:21
  101.7 11.6 %collective-permute-start.5 = (f32[32,2048]{1,0:T(8,128)S(1)}, f32[32,2048]{1,0:T(8,128)S(1)}, u32[]{:S(2)}, u32[]{:S(2)}) collective-permute-start(f32[32,2048]{1,0:T(8,128)S(1)} %divide_subtract_fusion.1), channel_id=1, source_target_pairs={{8,0},{16,8},{24,16},{32,24},{40,32},{48,40},{56,48},{64,56},{72,6... | collective-permute-start | bytes 786440 | tf_op jit(solution)/shard_map/ppermute | solution.py:24
  156.4 223.3 %all-reduce.6.cloned.1.call-start = ((), (), s32[]{:S(2)}) async-start(), calls=%async_computation.2 | async-start | bytes 524288 | tf_op jit(solution)/shard_map/psum | solution.py:9
  381.8 0.7 copy-start.3
  394.2 0.6 copy-start.4
  424.5 2.0 copy-start.2
Sparse Core Ops, SparseCore 0:
  156.5 152.8 all-reduce.3
  311.8 67.8 all-reduce.5
